TPU v7x, 128 devices: a whole 4x4x4 slice. The times are simulated.
128 devices in a mesh: seq: 16 (over z, y), head: 8 (over x, core).
Axes of the slice: x: 4, y: 4, z: 4, core: 2. Of those that a mesh axis runs over, the one named last changes fastest.
Arguments:
- normed: bfloat16 [32, 8192], P(None, 'seq'), may hold values from -6 to 6
- qkv_weight: bfloat16 [8192, 10240], P('seq', 'head'), may hold values from -0.0625 to 0.0625
- out_weight: bfloat16 [8192, 8192], P('head', 'seq'), may hold values from -0.0625 to 0.0625
- kv_cache: bfloat16 [1024, 2, 128, 1024], P('seq', None, None, 'head'), may hold values from -160 to 160
- lengths: int32 [8], replicated, may hold values from 1 to 9344, as said below
- slot_request: int32 [1024], P('seq'), may hold values from 0 to 8, as said below
- slot_block: int32 [1024], P('seq'), may hold values from 0 to 72, as said below
- send_list: int32 [16, 16, 4], P('seq'), may hold values from 0 to 64, as said below
- recv_list: int32 [16, 16, 4], P('seq'), may hold values from 0 to 64, as said below
Outputs:
- projected: bfloat16 [32, 8192], P('head', 'seq')
- moved_cache: bfloat16 [1024, 2, 128, 1024], P('seq', None, None, 'head')
Inputs may be any that keep to these rules, and one draw needn't show every extreme that they name: `lengths`: every request has at least one block; a request with n blocks has each of the block numbers 0 to n - 1 in exactly one slot, and its length lies in ((n - 1) * 128, n * 128]. `slot_request`: 8 marks an empty slot. `slot_block`: 0 in empty slots. 64 marks an unused entry, and send_list[s, e, c] is unused exactly where recv_list[e, s, c] is; every owned slot is sent exactly once and no empty slot is sent; at most 4 blocks go from one device to another, and some device receives exactly 4 from every device; after the scale-in only half of the seq devices hold blocks. `recv_list`: 64 marks an unused entry; each slot of a device is filled at most once.
All inputs are finite; a program needn't handle non-finite values.
Results may differ from a plain program's by a relative error of at most 0.025.
Values may be sent and summed in bfloat16 or wider, within the bound.
A program may use at most 128 MiB of HBM per device.

v0:
```python
import jax
import jax.numpy as jnp
from jax import lax
from jax.sharding import PartitionSpec as P

HEADS = 64
KV_HEADS = 8
HEAD = 128
POS = 4
BLOCK = 128
rope_base = 500000.0
neg_large = -1e30


def rotate(values, positions):
    half_width = values.shape[-1] // 2
    frequencies = rope_base ** (
        -(jnp.arange(half_width, dtype=jnp.float32) * 2.0 / values.shape[-1])
    )
    angles = positions[..., None] * frequencies
    cosine_table = jnp.cos(angles)
    sine_table = jnp.sin(angles)
    lower_half = values[..., :half_width]
    upper_half = values[..., half_width:]
    return jnp.concatenate(
        [
            lower_half * cosine_table - upper_half * sine_table,
            upper_half * cosine_table + lower_half * sine_table,
        ],
        axis=-1,
    )


def body(
    normed,
    qkv_weight,
    out_weight,
    kv_cache,
    lengths,
    slot_request,
    slot_block,
    send_list,
    recv_list,
):
    group_size = HEADS // KV_HEADS
    scale_factor = HEAD ** (-0.5)
    requests = lengths.shape[0]
    slot_count = kv_cache.shape[0]
    full_rows = lax.all_gather(normed, "seq", axis=1, tiled=True)
    projected_qkv = jnp.dot(
        full_rows,
        lax.all_gather(qkv_weight, "seq", axis=0, tiled=True),
        preferred_element_type=jnp.float32,
    )
    projected_qkv = projected_qkv.reshape(requests, POS, -1, group_size + 2, HEAD)
    local_kv = projected_qkv.shape[2]
    positions = (lengths[:, None] + jnp.arange(POS, dtype=jnp.int32)[None, :]).astype(jnp.float32)
    queries = rotate(projected_qkv[:, :, :, :group_size], positions[:, :, None, None]).astype(
        jnp.bfloat16
    )
    keys_new = rotate(projected_qkv[:, :, :, group_size], positions[:, :, None]).astype(
        jnp.bfloat16
    )
    values_new = projected_qkv[:, :, :, group_size + 1].astype(jnp.bfloat16)
    flat_send = send_list.reshape(-1)
    outgoing = kv_cache[jnp.minimum(flat_send, slot_count - 1)]
    outgoing = outgoing.reshape((lax.axis_size("seq"), -1) + kv_cache.shape[1:])
    incoming = lax.all_to_all(outgoing, "seq", split_axis=0, concat_axis=0, tiled=True)
    incoming = incoming.reshape((-1,) + kv_cache.shape[1:])
    moved_cache = jnp.zeros_like(kv_cache).at[recv_list.reshape(-1)].set(incoming, mode="drop")
    slot_clip = jnp.minimum(slot_request, requests - 1)
    live_slot = slot_request < requests
    token_pos = slot_block[:, None] * BLOCK + jnp.arange(BLOCK, dtype=jnp.int32)[None, :]
    token_valid = (token_pos < lengths[slot_clip][:, None]) & live_slot[:, None]
    cache_view = kv_cache.reshape(slot_count, 2, BLOCK, local_kv, HEAD)
    gathered = queries[slot_clip]
    scores = (
        jnp.einsum(
            "sptgd,sbtd->stgpb", gathered, cache_view[:, 0], preferred_element_type=jnp.float32
        )
        * scale_factor
    )
    scores = jnp.where(token_valid[:, None, None, None, :], scores, neg_large)
    slot_max = jnp.max(scores, axis=-1)
    weights = jnp.where(
        token_valid[:, None, None, None, :], jnp.exp(scores - slot_max[..., None]), 0.0
    )
    slot_sum = jnp.sum(weights, axis=-1)
    slot_acc = jnp.einsum(
        "stgpb,sbtd->stgpd",
        weights.astype(jnp.bfloat16),
        cache_view[:, 1],
        preferred_element_type=jnp.float32,
    )
    flat_width = local_kv * group_size * POS
    slot_max_flat = slot_max.reshape(slot_count, flat_width)
    member = slot_request[:, None] == jnp.arange(requests, dtype=jnp.int32)[None, :]
    request_max = jnp.max(
        jnp.where(member[:, None, :], slot_max_flat[:, :, None], neg_large), axis=0
    ).T
    rescale = jnp.exp(slot_max_flat - request_max[slot_clip])
    member_float = member.astype(jnp.float32).T
    request_sum = jnp.dot(
        member_float,
        slot_sum.reshape(slot_count, flat_width) * rescale,
        precision=lax.Precision.HIGHEST,
    )
    scaled_acc = (slot_acc.reshape(slot_count, flat_width, HEAD) * rescale[:, :, None]).reshape(
        slot_count, flat_width * HEAD
    )
    request_acc = jnp.dot(member_float, scaled_acc, precision=lax.Precision.HIGHEST).reshape(
        requests, flat_width, HEAD
    )
    total_max = lax.pmax(request_max, "seq")
    adjust = jnp.exp(request_max - total_max)
    total_sum, total_acc = (
        lax.psum((request_sum * adjust).astype(jnp.bfloat16), "seq").astype(jnp.float32),
        lax.psum((request_acc * adjust[:, :, None]).astype(jnp.bfloat16), "seq").astype(
            jnp.float32
        ),
    )
    new_scores = (
        jnp.einsum("rptgd,rqtd->rtgpq", queries, keys_new, preferred_element_type=jnp.float32)
        * scale_factor
    )
    causal = jnp.arange(POS)[:, None] >= jnp.arange(POS)[None, :]
    new_scores = jnp.where(causal, new_scores, neg_large)
    cache_max = total_max.reshape(requests, local_kv, group_size, POS)
    top_max = jnp.maximum(cache_max, jnp.max(new_scores, axis=-1))
    carry_scale = jnp.exp(cache_max - top_max)
    new_weights = jnp.where(causal, jnp.exp(new_scores - top_max[..., None]), 0.0)
    denominator = total_sum.reshape(requests, local_kv, group_size, POS) * carry_scale + jnp.sum(
        new_weights, axis=-1
    )
    numerator = (
        total_acc.reshape(requests, local_kv, group_size, POS, HEAD) * carry_scale[..., None]
    )
    numerator = numerator + jnp.einsum(
        "rtgpq,rqtd->rtgpd",
        new_weights.astype(jnp.bfloat16),
        values_new,
        preferred_element_type=jnp.float32,
    )
    attended = (
        (numerator / denominator[..., None])
        .transpose(0, 3, 1, 2, 4)
        .reshape(requests * POS, -1)
        .astype(jnp.bfloat16)
    )
    projected = lax.psum_scatter(
        jnp.dot(attended, out_weight, preferred_element_type=jnp.float32).astype(jnp.bfloat16),
        "head",
        scatter_dimension=0,
        tiled=True,
    )
    return (projected, moved_cache)


def solution(mesh):
    placed = (
        P(None, "seq"),
        P("seq", "head"),
        P("head", "seq"),
        P("seq", None, None, "head"),
        P(),
        P("seq"),
        P("seq"),
        P("seq", None, None),
        P("seq", None, None),
    )
    return jax.shard_map(
        body,
        mesh=mesh,
        in_specs=placed,
        out_specs=(P("head", "seq"), P("seq", None, None, "head")),
        check_vma=False,
    )
```

profile of v0, /device:TPU:0, one launch (start us, length us, event | category | flops | bytes accessed | tf_op | source)
XLA Modules:
  0.0 363.6 jit_solution(1940336600849006869)
XLA Ops:
  8.8 5.3 %gather_fusion.2 = bf16[64,2,128,128]{3,2,1,0:T(8,128)(2,1)} fusion(bf16[64,2,128,128]{3,2,1,0:T(8,128)(2,1)} %param.12, s32[1024]{0:T(1024)S(1)} %pad_clamp_fusion), kind=kCustom, calls=%fused_computation.2 | custom fusion | bytes 8388864 | tf_op jit(solution)/shard_map/gather | solution.py:66
  14.1 8.2 %all-to-all-start = ((bf16[16,4,2,128,128]{4,3,2,1,0:T(8,128)(2,1)}), bf16[16,4,2,128,128]{4,3,2,1,0:T(8,128)(2,1)}, u32[]{:S(2)}, u32[]{:S(2)}) async-start(bf16[16,4,2,128,128]{4,3,2,1,0:T(8,128)(2,1)} %bitcast.134), calls=%async_computation | async-start | bytes 8388608 | tf_op jit(solution)/shard_map/all_to_all | solution.py:68
  22.4 5.2 %copy.111 = bf16[64,2,128,128]{3,2,0,1:T(8,128)(2,1)} copy(bf16[64,2,128,128]{3,2,1,0:T(8,128)(2,1)} %param.12) | data formatting | bytes 8388608 | tf_op args[3]
  30.3 4.8 %compare_select_fusion.3 = (s32[64]{0:T(128)S(1)}, s32[64]{0:T(128)S(1)}, s32[64]{0:T(128)S(1)}) fusion(s32[]{:T(128)} %bitcast.1, s32[]{:T(128)} %bitcast.2, s32[]{:T(128)} %bitcast.3, s32[]{:T(128)} %bitcast.4, s32[]{:T(128)} %bitcast.5, s32[]{:T(128)} %bitcast.6, s32[]{:T(128)} %bitcast.7, s32[]{:T(128)} %bitcast.8, s32[64]{0:T(128)S(1)} %copy-done.7, ...), kind=kLoop, calls=%fused_computation.87 | loop fusion | flops 1216 | bytes 1312 | tf_op jit(solution)/shard_map/gather | solution.py:74
  35.2 80.1 %all_gather.6 = bf16[32,8192]{1,0:T(8,128)(2,1)S(1)} all-gather(bf16[32,512]{1,0:T(8,128)(2,1)S(1)} %copy-done.6), channel_id=1, replica_groups=mesh['seq'=16,'head'=8] {'seq'}, dimensions={1}, use_global_device_ids=true | all-gather | bytes 557056 | tf_op jit(solution)/shard_map/all_gather | solution.py:49
  115.7 3.1 broadcast_in_dim.96
  118.8 11.8 %scatter_fusion = bf16[64,2,128,128]{3,2,1,0:T(8,128)(2,1)} fusion(bf16[64,2,128,128]{3,2,1,0:T(8,128)(2,1)} %broadcast_in_dim.96, s32[64]{0:T(128)S(1)} %fusion.49, bf16[64,2,128,128]{3,2,1,0:T(8,128)(2,1)} %bitcast.45), kind=kCustom, calls=%fused_computation.3 | custom fusion | bytes 12583168 | tf_op jit(solution)/shard_map/scatter | solution.py:70
  130.6 61.3 %all-gather.2.cloned.1.call-done = bf16[8192,1280]{1,0:T(8,128)(2,1)} async-done(((bf16[512,1280]{1,0:T(8,128)(2,1)}), bf16[8192,1280]{1,0:T(8,128)(2,1)}) %all-gather.2.cloned.1.call-update) | async-done | bytes 20971536 | tf_op jit(solution)/shard_map/all_gather | solution.py:52
  191.9 8.8 %fusion.56 = f32[32,1280]{1,0:T(8,128)S(1)} fusion(bf16[32,8192]{1,0:T(8,128)(2,1)S(1)} %all_gather.6, bf16[8192,1280]{1,0:T(8,128)(2,1)} %all-gather.2.cloned.1.call-done), kind=kOutput, calls=%fused_computation.106 | convolution fusion | flops 671088640 | bytes 21659648 | tf_op jit(solution)/shard_map/dot_general | solution.py:50
  201.6 2.9 fusion.54
  205.5 38.1 %pmax.7 = f32[8,32]{1,0:T(8,128)S(1)} all-reduce(f32[8,32]{1,0:T(8,128)S(1)} %bitcast.130), channel_id=1, replica_groups=mesh['seq'=16,'head'=8] {'seq'}, use_global_device_ids=true, to_apply=%region_2.3 | all-reduce | flops 256 | bytes 2048 | tf_op jit(solution)/shard_map/pmax | solution.py:114
  243.7 1.2 gather_fusion.1
  246.3 0.8 fusion.15
  247.0 2.3 fusion
  249.7 0.8 subtract_exponential_fusion
  250.9 1.8 fusion.7
  253.3 0.9 fusion.45
  254.2 0.8 copy.73
  255.2 0.8 fusion.11
  256.2 36.0 %psum.15 = bf16[8,8,4]{1,2,0:T(4,128)(2,1)S(1)} all-reduce(bf16[8,8,4]{1,2,0:T(4,128)(2,1)S(1)} %copy.79), channel_id=1, replica_groups=mesh['seq'=16,'head'=8] {'seq'}, use_global_device_ids=true, to_apply=%region_6.7 | all-reduce | flops 256 | bytes 1024 | tf_op jit(solution)/shard_map/psum | solution.py:117
  292.2 1.4 fusion.55
  293.8 36.9 %all-reduce.3.cloned.1.call-done = bf16[8,8,4,128]{3,1,2,0:T(8,128)(2,1)} async-done(((bf16[8,8,4,128]{3,1,2,0:T(8,128)(2,1)}), bf16[8,8,4,128]{3,1,2,0:T(8,128)(2,1)}) %all-reduce.3.cloned.1.call-update) | async-done | bytes 65552 | tf_op jit(solution)/shard_map/psum | solution.py:118
  330.7 1.1 fusion.8
  332.1 24.0 %all-reduce = bf16[32,512]{1,0:T(8,128)(2,1)S(1)} all-reduce(bf16[32,512]{1,0:T(8,128)(2,1)S(1)} %convolution_convert_fusion), channel_id=2, replica_groups=mesh['seq'=16,'head'=8] {'head'}, use_global_device_ids=true, to_apply=%region_8.9.clone | all-reduce | flops 16384 | bytes 65536
  (75 shorter events, 10.2 us)
Async XLA Ops:
  7.2 324.7 %copy-start = (bf16[1024,512]{1,0:T(8,128)(2,1)S(1)}, bf16[1024,512]{1,0:T(8,128)(2,1)}, u32[]{:S(2)}) copy-start(bf16[1024,512]{1,0:T(8,128)(2,1)} %param.11) | copy-start | bytes 3145732
  7.2 184.7 %all-gather.2.cloned.1.call-start = ((), (), s32[]{:S(2)}) async-start(), calls=%async_computation.1 | async-start | bytes 22282240 | tf_op jit(solution)/shard_map/all_gather | solution.py:52
  14.1 101.6 %all-to-all-start = ((bf16[16,4,2,128,128]{4,3,2,1,0:T(8,128)(2,1)}), bf16[16,4,2,128,128]{4,3,2,1,0:T(8,128)(2,1)}, u32[]{:S(2)}, u32[]{:S(2)}) async-start(bf16[16,4,2,128,128]{4,3,2,1,0:T(8,128)(2,1)} %bitcast.134), calls=%async_computation | async-start | bytes 8388608 | tf_op jit(solution)/shard_map/all_to_all | solution.py:68
  22.3 5.3 %copy-start.9 = (s32[1,16,4]{1,2,0:T(4,128)S(1)}, s32[1,16,4]{1,2,0:T(4,128)}, u32[]{:S(2)}) copy-start(s32[1,16,4]{1,2,0:T(4,128)} %param.17) | copy-start | bytes 772
  22.3 5.5 %copy-start.12 = (u32[128]{0:T(128)S(1)}, u32[128]{0:T(128)}, u32[]{:S(2)}) copy-start(u32[128]{0:T(128)} %constant.43) | copy-start | bytes 1540
  22.3 7.4 %copy-start.3 = (s32[8]{0:T(128)S(1)}, s32[8]{0:T(128)}, u32[]{:S(2)}) copy-start(s32[8]{0:T(128)} %param.13) | copy-start | bytes 100
  22.3 8.0 %copy-start.7 = (s32[64]{0:T(128)S(1)}, s32[64]{0:T(128)}, u32[]{:S(2)}) copy-start(s32[64]{0:T(128)} %param.14) | copy-start | bytes 772
  22.3 8.0 %copy-start.11 = (s32[64]{0:T(128)S(1)}, s32[64]{0:T(128)}, u32[]{:S(2)}) copy-start(s32[64]{0:T(128)} %param.15) | copy-start | bytes 772
  22.3 12.8 %copy-start.6 = (bf16[32,512]{1,0:T(8,128)(2,1)S(1)}, bf16[32,512]{1,0:T(8,128)(2,1)}, u32[]{:S(2)}) copy-start(bf16[32,512]{1,0:T(8,128)(2,1)} %param.9) | copy-start | bytes 98308
  22.4 308.4 %all-reduce.3.cloned.1.call-start = ((), (), s32[]{:S(2)}) async-start(), calls=%async_computation.2 | async-start | bytes 131072 | tf_op jit(solution)/shard_map/psum | solution.py:118
  29.1 101.5 %copy-start.8 = (f32[64]{0:T(128)}, f32[64]{0:T(128)S(1)}, u32[]{:S(2)}) copy-start(f32[64]{0:T(128)S(1)} %negate_power_fusion) | copy-start | bytes 772
  115.4 15.2 %copy-start.5 = (f32[8,4]{1,0:T(8,128)}, f32[8,4]{1,0:T(8,128)S(1)}, u32[]{:S(2)}) copy-start(f32[8,4]{1,0:T(8,128)S(1)} %add_convert_fusion.1) | copy-start | bytes 388
  200.8 0.8 copy-start.1
  200.9 0.8 copy-start.2
  244.9 2.1 copy-start.4
  249.7 43.9 %copy-start.10 = (pred[4,4]{1,0:T(4,128)(4,1)S(1)}, pred[4,4]{1,0:T(4,128)(4,1)}, u32[]{:S(2)}) copy-start(pred[4,4]{1,0:T(4,128)(4,1)} %iota_compare_fusion.3) | copy-start | bytes 52
Sparse Core Ops, SparseCore 0:
  10.1 181.6 all-gather.1
  253.4 77.2 all-reduce.2
where the time goes:
time: 365 us; the launch traced here: 364 us
  blocking collectives  178 us (49%)
  waiting for transfers between devices  98.9 us (27%)
  local copies, waits for them, and re-layouts  34.3 us (9%)
  matrix products  19.4 us (5%)
  between operations  15.1 us (4%)
  other arithmetic  9.38 us (3%)
  starting transfers between devices  8.26 us (2%)
    all_gather x1, blocking collectives, body(): full_rows = lax.all_gather(normed, 'seq', axis=1, tiled=True)  80.1 us
    all_gather x1, waiting for transfers between devices, body(): lax.all_gather(qkv_weight, 'seq', axis=0, tiled=True)  61.3 us
    pmax x1, blocking collectives, body(): total_max = lax.pmax(request_max, 'seq')  38.1 us
    psum x1, waiting for transfers between devices, body(): lax.psum((request_acc * adjust[:, :, None]).astype(jnp.bfloat16), 'seq')  36.9 us
    psum x1, blocking collectives, body(): lax.psum((request_sum * adjust).astype(jnp.bfloat16), 'seq')  36 us
    unnamed x1, blocking collectives  24 us
    scatter x1, local copies, waits for them, and re-layouts, body(): jnp.zeros_like(kv_cache).at[recv_list.reshape(-1)]  11.8 us
    dot_general x1, matrix products, body(): jnp.dot(full_rows, lax.all_gather(qkv_weight, 'seq', axis=0, tiled=True),...  8.79 us
  transfers between devices with their start and end apart: 3, of which 2 were waited for; matrix products, arithmetic and copies ran while one was open for 10% of the time, Pallas kernels for 0%

commit v1 on v0

--- a/solution.py
+++ b/solution.py
@@ -46,7 +46,9 @@
     scale_factor = HEAD ** (-0.5)
     requests = lengths.shape[0]
     slot_count = kv_cache.shape[0]
-    full_rows = lax.all_gather(normed, "seq", axis=1, tiled=True)
+    full_rows = jnp.concatenate(
+        lax.all_to_all(jnp.stack([normed] * lax.axis_size("seq")), "seq", 0, 0), axis=1
+    )
     projected_qkv = jnp.dot(
         full_rows,
         lax.all_gather(qkv_weight, "seq", axis=0, tiled=True),

time: 365 us -> 388 us (1.063)
  blocking collectives: 178 us -> 97.5 us
  waiting for transfers between devices: 98.9 us -> 175 us
  local copies, waits for them, and re-layouts: 34.3 us -> 59.8 us
  starting transfers between devices: 8.26 us -> 12.8 us
    all_gather x1 -> x0, blocking collectives: 80.1 us -> none  [body(): full_rows = lax.all_gather(normed, 'seq', axis=1, tiled=True)]
    all_to_all x1, waiting for transfers between devices: 0.01 us -> 60.3 us  [body(): lax.all_to_all(outgoing, 'seq', split_axis=0, concat_axis=0, tiled=True)]
    dot_general x0 -> x2, local copies, waits for them, and re-layouts: none -> 27.3 us  [body(): jnp.dot(full_rows, lax.all_gather(qkv_weight, 'seq', axis=0, tiled=True),...]
    all_gather x1, waiting for transfers between devices: 61.3 us -> 69.7 us  [body(): lax.all_gather(qkv_weight, 'seq', axis=0, tiled=True)]
    all_to_all x0 -> x1, starting transfers between devices: none -> 8.15 us  [body(): lax.all_to_all(jnp.stack([normed] * lax.axis_size('seq')), 'seq', 0, 0)]
    all_to_all x0 -> x1, waiting for transfers between devices: none -> 5.45 us  [body(): lax.all_to_all(jnp.stack([normed] * lax.axis_size('seq')), 'seq', 0, 0)]
  transfers between devices with their start and end apart: 3 -> 4, of which waited for: 2 -> 4; matrix products, arithmetic and copies ran while one was open for 10% -> 9% of each run, Pallas kernels for 0% -> 0%
where the time goes in v1:
time: 388 us; the launch traced here: 387 us
  waiting for transfers between devices  175 us (45%)
  blocking collectives  97.5 us (25%)
  local copies, waits for them, and re-layouts  59.8 us (15%)
  matrix products  18.8 us (5%)
  between operations  15 us (4%)
  starting transfers between devices  12.8 us (3%)
  other arithmetic  7.6 us (2%)
    all_gather x1, waiting for transfers between devices, body(): lax.all_gather(qkv_weight, 'seq', axis=0, tiled=True)  69.7 us
    all_to_all x1, waiting for transfers between devices, body(): lax.all_to_all(outgoing, 'seq', split_axis=0, concat_axis=0, tiled=True)  60.3 us
    psum x1, waiting for transfers between devices, body(): lax.psum((request_acc * adjust[:, :, None]).astype(jnp.bfloat16), 'seq')  39.3 us
    psum x1, blocking collectives, body(): lax.psum((request_sum * adjust).astype(jnp.bfloat16), 'seq')  37.3 us
    pmax x1, blocking collectives, body(): total_max = lax.pmax(request_max, 'seq')  36.1 us
    dot_general x2, local copies, waits for them, and re-layouts, body(): jnp.dot(full_rows, lax.all_gather(qkv_weight, 'seq', axis=0, tiled=True),...  27.3 us
    unnamed x1, blocking collectives  24 us
    scatter x1, local copies, waits for them, and re-layouts, body(): jnp.zeros_like(kv_cache).at[recv_list.reshape(-1)]  11.8 us
  transfers between devices with their start and end apart: 4, of which 4 were waited for; matrix products, arithmetic and copies ran while one was open for 9% of the time, Pallas kernels for 0%

profile of v1, /device:TPU:0, one launch (start us, length us, event | category | flops | bytes accessed | tf_op | source)
XLA Modules:
  0.0 387.0 jit_solution(7113714042065067603)
XLA Ops:
  7.2 0.7 all-gather.2.cloned.1.call-update
  7.9 1.6 stack.2
  9.5 8.1 %all-to-all-start = ((bf16[16,32,512]{2,1,0:T(8,128)(2,1)}), bf16[16,32,512]{2,1,0:T(8,128)(2,1)S(1)}, u32[]{:S(2)}, u32[]{:S(2)}) async-start(bf16[16,32,512]{2,1,0:T(8,128)(2,1)} %stack.2), calls=%async_computation | async-start | bytes 1048576 | tf_op jit(solution)/shard_map/all_to_all | solution.py:50
  17.7 0.7 broadcast_minimum_fusion
  18.6 5.3 %gather_fusion.2 = bf16[64,2,128,128]{3,2,1,0:T(8,128)(2,1)} fusion(bf16[64,2,128,128]{3,2,1,0:T(8,128)(2,1)} %param.12, s32[1024]{0:T(1024)S(1)} %pad_clamp_fusion), kind=kCustom, calls=%fused_computation.2 | custom fusion | bytes 8388864 | tf_op jit(solution)/shard_map/gather | solution.py:68
  23.8 5.4 %all-to-all-done = bf16[16,32,512]{2,1,0:T(8,128)(2,1)S(1)} async-done(((bf16[16,32,512]{2,1,0:T(8,128)(2,1)}), bf16[16,32,512]{2,1,0:T(8,128)(2,1)S(1)}, u32[]{:S(2)}, u32[]{:S(2)}) %all-to-all-start) | async-done | bytes 524320 | tf_op jit(solution)/shard_map/all_to_all | solution.py:50
  29.3 4.5 %all-to-all-start.1 = ((bf16[16,4,2,128,128]{4,3,2,1,0:T(8,128)(2,1)}), bf16[16,4,2,128,128]{4,3,2,1,0:T(8,128)(2,1)}, u32[]{:S(2)}, u32[]{:S(2)}) async-start(bf16[16,4,2,128,128]{4,3,2,1,0:T(8,128)(2,1)} %bitcast.146), calls=%async_computation.1 | async-start | bytes 8388608 | tf_op jit(solution)/shard_map/all_to_all | solution.py:70
  34.0 4.8 %copy.120 = bf16[64,2,128,128]{3,2,0,1:T(8,128)(2,1)} copy(bf16[64,2,128,128]{3,2,1,0:T(8,128)(2,1)} %param.12) | data formatting | bytes 8388608 | tf_op args[3]
  40.9 4.9 %compare_select_fusion.3 = (s32[64]{0:T(128)S(1)}, s32[64]{0:T(128)S(1)}, s32[64]{0:T(128)S(1)}) fusion(s32[]{:T(128)} %bitcast.1, s32[]{:T(128)} %bitcast.2, s32[]{:T(128)} %bitcast.3, s32[]{:T(128)} %bitcast.4, s32[]{:T(128)} %bitcast.5, s32[]{:T(128)} %bitcast.6, s32[]{:T(128)} %bitcast.7, s32[]{:T(128)} %bitcast.8, s32[64]{0:T(128)S(1)} %copy-done.3, ...), kind=kLoop, calls=%fused_computation.88 | loop fusion | flops 1216 | bytes 1312 | tf_op jit(solution)/shard_map/gather | solution.py:76
  46.9 60.3 %all-to-all-done.1 = bf16[16,4,2,128,128]{4,3,2,1,0:T(8,128)(2,1)} async-done(((bf16[16,4,2,128,128]{4,3,2,1,0:T(8,128)(2,1)}), bf16[16,4,2,128,128]{4,3,2,1,0:T(8,128)(2,1)}, u32[]{:S(2)}, u32[]{:S(2)}) %all-to-all-start.1) | async-done | bytes 4194336 | tf_op jit(solution)/shard_map/all_to_all | solution.py:70
  107.2 3.1 broadcast_in_dim.96
  110.3 11.8 %scatter_fusion = bf16[64,2,128,128]{3,2,1,0:T(8,128)(2,1)} fusion(bf16[64,2,128,128]{3,2,1,0:T(8,128)(2,1)} %broadcast_in_dim.96, s32[64]{0:T(128)S(1)} %fusion.49, bf16[64,2,128,128]{3,2,1,0:T(8,128)(2,1)} %bitcast.52), kind=kCustom, calls=%fused_computation.3 | custom fusion | bytes 12583168 | tf_op jit(solution)/shard_map/scatter | solution.py:72
  122.0 69.7 %all-gather.2.cloned.1.call-done = bf16[8192,1280]{1,0:T(8,128)(2,1)} async-done(((bf16[512,1280]{1,0:T(8,128)(2,1)}), bf16[8192,1280]{1,0:T(8,128)(2,1)}) %all-gather.2.cloned.1.call-update) | async-done | bytes 20971536 | tf_op jit(solution)/shard_map/all_gather | solution.py:54
  191.7 26.9 %copy.72 = bf16[1280,8192]{1,0:T(8,128)(2,1)} copy(bf16[1280,8192]{0,1:T(8,128)(2,1)} %bitcast.140) | data formatting | bytes 41943040 | tf_op jit(solution)/shard_map/dot_general | solution.py:52
  218.7 10.6 %convolution_bitcast_fusion = f32[8,4,1,10,128]{4,1,3,0,2:T(4,128)S(1)} fusion(bf16[10,128,8192,1]{2,1,0,3:T(8,128)(2,1)} %bitcast.141, bf16[8,4,8192,1]{2,1,0,3:T(4,128)(2,1)S(1)} %reshape.494), kind=kOutput, calls=%fused_computation.13 | convolution fusion | flops 671088640 | bytes 21659648 | tf_op jit(solution)/shard_map/dot_general | solution.py:52
  230.2 2.9 fusion.54
  233.5 36.1 %pmax.7 = f32[8,32]{1,0:T(8,128)S(1)} all-reduce(f32[8,32]{1,0:T(8,128)S(1)} %bitcast.142), channel_id=1, replica_groups=mesh['seq'=16,'head'=8] {'seq'}, use_global_device_ids=true, to_apply=%region_2.3 | all-reduce | flops 256 | bytes 2048 | tf_op jit(solution)/shard_map/pmax | solution.py:116
  270.4 0.8 fusion.15
  271.2 2.3 fusion
  274.2 1.1 fusion.7
  276.8 37.3 %psum.15 = bf16[8,8,4]{1,2,0:T(4,128)(2,1)S(1)} all-reduce(bf16[8,8,4]{1,2,0:T(4,128)(2,1)S(1)} %copy.89), channel_id=1, replica_groups=mesh['seq'=16,'head'=8] {'seq'}, use_global_device_ids=true, to_apply=%region_6.7 | all-reduce | flops 256 | bytes 1024 | tf_op jit(solution)/shard_map/psum | solution.py:119
  314.8 39.3 %all-reduce.3.cloned.1.call-done = bf16[8,8,4,128]{3,1,2,0:T(8,128)(2,1)} async-done(((bf16[8,8,4,128]{3,1,2,0:T(8,128)(2,1)}), bf16[8,8,4,128]{3,1,2,0:T(8,128)(2,1)}) %all-reduce.3.cloned.1.call-update) | async-done | bytes 65552 | tf_op jit(solution)/shard_map/psum | solution.py:120
  354.1 1.1 fusion.8
  355.5 24.0 %all-reduce = bf16[32,512]{1,0:T(8,128)(2,1)S(1)} all-reduce(bf16[32,512]{1,0:T(8,128)(2,1)S(1)} %convolution_convert_fusion), channel_id=2, replica_groups=mesh['seq'=16,'head'=8] {'head'}, use_global_device_ids=true, to_apply=%region_8.9.clone | all-reduce | flops 16384 | bytes 65536
  (67 shorter events, 8.7 us)
Async XLA Ops:
  7.2 348.1 %copy-start = (bf16[1024,512]{1,0:T(8,128)(2,1)S(1)}, bf16[1024,512]{1,0:T(8,128)(2,1)}, u32[]{:S(2)}) copy-start(bf16[1024,512]{1,0:T(8,128)(2,1)} %param.11) | copy-start | bytes 3145732
  7.2 184.6 %all-gather.2.cloned.1.call-start = ((), (), s32[]{:S(2)}) async-start(), calls=%async_computation.2 | async-start | bytes 22282240 | tf_op jit(solution)/shard_map/all_gather | solution.py:54
  9.5 19.8 %all-to-all-start = ((bf16[16,32,512]{2,1,0:T(8,128)(2,1)}), bf16[16,32,512]{2,1,0:T(8,128)(2,1)S(1)}, u32[]{:S(2)}, u32[]{:S(2)}) async-start(bf16[16,32,512]{2,1,0:T(8,128)(2,1)} %stack.2), calls=%async_computation | async-start | bytes 1048576 | tf_op jit(solution)/shard_map/all_to_all | solution.py:50
  29.3 77.9 %all-to-all-start.1 = ((bf16[16,4,2,128,128]{4,3,2,1,0:T(8,128)(2,1)}), bf16[16,4,2,128,128]{4,3,2,1,0:T(8,128)(2,1)}, u32[]{:S(2)}, u32[]{:S(2)}) async-start(bf16[16,4,2,128,128]{4,3,2,1,0:T(8,128)(2,1)} %bitcast.146), calls=%async_computation.1 | async-start | bytes 8388608 | tf_op jit(solution)/shard_map/all_to_all | solution.py:70
  33.8 4.9 %copy-start.4 = (s32[1,16,4]{1,2,0:T(4,128)S(1)}, s32[1,16,4]{1,2,0:T(4,128)}, u32[]{:S(2)}) copy-start(s32[1,16,4]{1,2,0:T(4,128)} %param.17) | copy-start | bytes 772
  33.9 5.1 %copy-start.6 = (u32[128]{0:T(128)S(1)}, u32[128]{0:T(128)}, u32[]{:S(2)}) copy-start(u32[128]{0:T(128)} %constant.43) | copy-start | bytes 1540
  33.9 6.3 %copy-start.2 = (s32[8]{0:T(128)S(1)}, s32[8]{0:T(128)}, u32[]{:S(2)}) copy-start(s32[8]{0:T(128)} %param.13) | copy-start | bytes 100
  33.9 7.0 %copy-start.3 = (s32[64]{0:T(128)S(1)}, s32[64]{0:T(128)}, u32[]{:S(2)}) copy-start(s32[64]{0:T(128)} %param.14) | copy-start | bytes 772
  33.9 7.0 %copy-start.5 = (s32[64]{0:T(128)S(1)}, s32[64]{0:T(128)}, u32[]{:S(2)}) copy-start(s32[64]{0:T(128)} %param.15) | copy-start | bytes 772
  33.9 320.2 %all-reduce.3.cloned.1.call-start = ((), (), s32[]{:S(2)}) async-start(), calls=%async_computation.3 | async-start | bytes 131072 | tf_op jit(solution)/shard_map/psum | solution.py:120
  229.2 41.9 %copy-start.1 = (f32[8,4,1,10,128]{4,1,3,0,2:T(4,128)}, f32[8,4,1,10,128]{4,1,3,0,2:T(4,128)S(1)}, u32[]{:S(2)}) copy-start(f32[8,4,1,10,128]{4,1,3,0,2:T(4,128)S(1)} %convolution_bitcast_fusion) | copy-start | bytes 491524
Sparse Core Ops, SparseCore 0:
  10.1 181.5 all-gather.1
  276.1 77.9 all-reduce.2
